TPU v7x, 32 devices: a whole 2x2x4 slice. The times are simulated.
32 devices in a mesh: cand: 16 (over z, x, core), tp: 2 (over y).
Axes of the slice: x: 2, y: 2, z: 4, core: 2. Of those that a mesh axis runs over, the one named last changes fastest.
Arguments:
- hidden_in: bfloat16 [128, 2, 8192], P('cand'), may hold values from -4 to 4
- queries: bfloat16 [128, 2, 32, 128], P('cand', None, 'tp'), may hold values from -128 to 128
- new_kv: bfloat16 [128, 2, 8, 2, 128], P('cand', None, 'tp'), may hold values from -5 to 5
- kv_cache: bfloat16 [128, 8, 2, 512, 128], P('cand', 'tp'), may hold values from -6 to 6
- lengths: int32 [128], P('cand'), may hold values from 128 to 512, as said below
- winner: int32 [8], replicated, may hold values from 0 to 15
- out_values: bfloat16 [4096, 8192], P('tp'), may hold values from -4 to 4
- out_scales: float32 [32, 64], P('tp'), may hold values from 0.008 to 0.032
Outputs:
- mixed: bfloat16 [128, 2, 8192], P('cand')
Inputs may be any that keep to these rules, and one draw needn't show every extreme that they name: `lengths`: every draw has some row with exactly 512 live slots.
All inputs are finite; a program needn't handle non-finite values.
Results may differ from a plain program's by a relative error of at most 0.013.
Values may be sent and summed in bfloat16 or wider, within the bound.
A program may use at most 128 MiB of HBM per device.

v0:
```python
import functools
import math

import jax
import jax.numpy as jnp
from jax import lax
from jax.experimental import pallas as pl
from jax.experimental.pallas import tpu as pltpu
from jax.sharding import PartitionSpec as P

BLOCK = 64
WINDOW = 128
LAG = 4
PAD = 16
LOW = -1e30
MESH = pl.DeviceIdType.MESH


def pick_kernel(lengths, winner, cache_hbm, blocks, held, sem):
    problems, kv_here, _, window, _ = held.shape
    slots = cache_hbm.shape[3]
    hs = blocks.shape[1]
    split = kv_here // hs
    me = lax.axis_index("cand")

    def begin_of(p):
        begin = lengths[p] - BLOCK
        base = jnp.clip(lax.div(begin, PAD) * PAD, 0, slots - window)
        return begin, pl.multiple_of(base, PAD)

    def fetch(p):
        base = begin_of(p)[1]
        return pltpu.make_async_copy(
            cache_hbm.at[p, :, :, pl.ds(base, window), :], held.at[p], sem.at[p]
        )

    for p in range(problems):
        fetch(p).start()
    row = lax.broadcasted_iota(jnp.int32, (BLOCK, window), 0)
    col = lax.broadcasted_iota(jnp.int32, (BLOCK, window), 1)
    for p in range(problems):
        fetch(p).wait()
        begin, base = begin_of(p)
        shift = jnp.where(winner[p] == me, begin - base, 4 * window)
        pick = (col == row + shift).astype(jnp.float32).astype(jnp.bfloat16)
        for h in range(kv_here):
            for kv in range(2):
                blocks[p * split + h // hs, h % hs, kv] = jnp.dot(
                    pick, held[p, h, kv], preferred_element_type=jnp.float32
                ).astype(jnp.bfloat16)


def kernel(
    cand_n, tp_n, tile, split,
    lengths, scales, blocks, queries, fresh, hidden, cache_hbm, weights_hbm, out,
    cache, weights, got, own, near0, up0, far0, down0, mid, near1, up1, far1, down1,
    fork, top_s, sum_s, acc_s, att, lhs, parts, other,
    cache_sem, weight_sem, send_sem, recv_sem, part_send, part_recv, swap_sem, other_send,
):
    me = lax.axis_index("cand")
    tp_me = lax.axis_index("tp")
    problems, kv_here, _, slots, head_dim = cache.shape
    steps_heads = queries.shape[1]
    heads = weights.shape[0] // head_dim
    steps = steps_heads // heads
    group = heads // kv_here
    rows = problems * steps
    half = problems // 2
    hs = kv_here // split
    chunks = half * split
    core = lax.rem(me, 2)
    chip = lax.div(me, 2)
    outer_len = 4
    inner_len = cand_n // 2 // outer_len
    inner_at = lax.rem(chip, inner_len)
    outer_at = lax.div(chip, inner_len)
    sibling = me + 1 - 2 * core

    def ends(at, length, stride):
        low_side = at < length // 2
        step = jnp.where(low_side, stride, -stride)
        has_near = jnp.logical_and(at > 0, at < length - 1)
        crosses = jnp.logical_or(at == length // 2 - 1, at == length // 2)
        return has_near, crosses, me + step, me - step

    inner = ends(inner_at, inner_len, 2)
    outer = ends(outer_at, outer_len, 2 * inner_len)

    barrier = pltpu.get_barrier_semaphore()

    def greet(**where):
        pl.semaphore_signal(barrier, inc=1, device_id=where, device_id_type=MESH)

    greet(cand=sibling)
    count = 1 + 2 * (tp_n - 1)
    for has_near, _, far, near in (inner, outer):
        greet(cand=far)

        @pl.when(has_near)
        def _(near=near):
            greet(cand=near)

        count = count + 1 + has_near.astype(jnp.int32)
    for k in range(1, tp_n):
        greet(tp=lax.rem(tp_me + k, tp_n))
        greet(cand=sibling, tp=lax.rem(tp_me + k, tp_n))

    pieces = weight_sem.shape[0]
    piece = weights.shape[0] // pieces

    def cache_copy(p):
        return pltpu.make_async_copy(cache_hbm.at[p], cache.at[p], cache_sem.at[p])

    def weight_copy(i):
        at = pl.ds(i * piece, piece)
        columns = pl.ds(pl.multiple_of(core * weights.shape[1], tile), weights.shape[1])
        return pltpu.make_async_copy(weights_hbm.at[at, columns], weights.at[at], weight_sem.at[i])

    for p in range(problems):
        cache_copy(p).start()
    pl.semaphore_wait(barrier, count)

    def remote(src, dst, kind, j, target):
        return pltpu.make_async_remote_copy(
            src_ref=src, dst_ref=dst, send_sem=send_sem.at[kind, j],
            recv_sem=recv_sem.at[kind, j], device_id={"cand": target}, device_id_type=MESH,
        )

    def sibling_copy(j):
        return remote(blocks.at[(1 - core) * chunks + j], got.at[j], 0, j, sibling)

    def loop(body, length):
        def step(j, carry):
            body(j)
            return carry

        lax.fori_loop(0, length, step, 0)

    loop(lambda j: sibling_copy(j).start(), chunks)

    def make_line(line, kind, base_ref, near_ref, up_ref, far_ref, down_ref):
        has_near, crosses, far_id, near_id = line

        def to_far_in(j):
            return remote(up_ref.at[j], near_ref.at[j], kind, j, far_id)

        def to_far_cross(j):
            return remote(up_ref.at[j], far_ref.at[j], kind + 1, j, far_id)

        def to_near(j):
            return remote(down_ref.at[j], far_ref.at[j], kind + 1, j, near_id)

        def climb(j):
            @pl.when(has_near)
            def _():
                to_far_in(j).wait_recv()
                up_ref[j] = base_ref[j] + near_ref[j]

            @pl.when(jnp.logical_not(has_near))
            def _():
                up_ref[j] = base_ref[j]

            @pl.when(crosses)
            def _():
                to_far_cross(j).start()

            @pl.when(jnp.logical_not(crosses))
            def _():
                to_far_in(j).start()

        def settle(j):
            to_far_cross(j).wait_recv()

            @pl.when(has_near)
            def _():
                down_ref[j] = base_ref[j] + far_ref[j]
                pltpu.make_async_remote_copy(
                    src_ref=down_ref.at[j], dst_ref=far_ref.at[j], send_sem=send_sem.at[kind + 2, j],
                    recv_sem=recv_sem.at[kind + 1, j], device_id={"cand": near_id}, device_id_type=MESH,
                ).start()

            return up_ref[j] + far_ref[j]

        def drain(j):
            @pl.when(crosses)
            def _():
                to_far_cross(j).wait_send()

            @pl.when(jnp.logical_not(crosses))
            def _():
                to_far_in(j).wait_send()

            @pl.when(has_near)
            def _():
                remote(down_ref.at[j], far_ref.at[j], kind + 2, j, near_id).wait_send()

        return climb, settle, drain

    climb0, settle0, drain0 = make_line(inner, 1, own, near0, up0, far0, down0)
    climb1, settle1, drain1 = make_line(outer, 4, mid, near1, up1, far1, down1)

    def enter(j):
        sibling_copy(j).wait_recv()
        own[j] = blocks[core * chunks + j] + got[j]
        climb0(j)

    loop(enter, chunks)
    for i in range(pieces):
        weight_copy(i).start()

    factor = 1.0 / math.sqrt(head_dim)

    def row_of(width):
        return lax.broadcasted_iota(jnp.int32, (steps_heads, width), 0)

    def col_of(width):
        return lax.broadcasted_iota(jnp.int32, (steps_heads, width), 1)

    def score(q, keys):
        return lax.dot_general(q, keys, (((1,), (1,)), ((), ())), preferred_element_type=jnp.float32) * factor

    def local_part(p):
        cache_copy(p).wait()
        q = queries[p]
        s = score(q, cache[p, :, 0].reshape(kv_here * slots, head_dim))
        row, col = row_of(kv_here * slots), col_of(kv_here * slots)
        mine = lax.div(lax.rem(row, heads), group) == lax.div(col, slots)
        s = jnp.where(jnp.logical_and(mine, lax.rem(col, slots) < lengths[p] - BLOCK), s, LOW)
        n = score(q, fresh[p, 0])
        width = fresh.shape[2]
        row, col = row_of(width), col_of(width)
        mine = lax.div(lax.rem(row, heads), group) == lax.div(col, steps)
        n = jnp.where(jnp.logical_and(mine, lax.rem(col, steps) <= lax.div(row, heads)), n, LOW)
        top = jnp.maximum(jnp.max(s, 1, keepdims=True), jnp.max(n, 1, keepdims=True))
        s = jnp.exp(s - top)
        n = jnp.exp(n - top)
        top_s[p] = jnp.broadcast_to(top, (steps_heads, head_dim))
        sum_s[p] = jnp.broadcast_to(jnp.sum(s, 1, keepdims=True) + jnp.sum(n, 1, keepdims=True), (steps_heads, head_dim))
        acc_s[p] = jnp.dot(
            s.astype(jnp.bfloat16), cache[p, :, 1].reshape(kv_here * slots, head_dim),
            preferred_element_type=jnp.float32,
        ) + jnp.dot(n.astype(jnp.bfloat16), fresh[p, 1], preferred_element_type=jnp.float32)

    def turn(j):
        mid[j] = settle0(j)
        climb1(j)


    def fork_copy(j):
        at = core * chunks + j
        return remote(fork.at[at], fork.at[at], 7, j, sibling)

    def finish(j):
        fork[core * chunks + j] = settle1(j)
        fork_copy(j).start()

    each = pl.cdiv(problems, chunks)

    def advance(j):
        @pl.when(j < chunks)
        def _():
            turn(j)

        for i in range(each):
            @pl.when(j * each + i < problems)
            def _(i=i):
                local_part(j * each + i)

        @pl.when(jnp.logical_and(j >= lag, j < chunks + lag))
        def _():
            finish(j - lag)

    lag = jnp.where(outer[0], LAG, chunks)
    loop(advance, 2 * chunks)

    def closing(j):
        remote(got.at[j], fork.at[(1 - core) * chunks + j], 7, j, sibling).wait_recv()

    loop(closing, chunks)

    def fork_part(p, carry):
        q = queries[p]
        both = fork[pl.ds(p * split, split)]
        keys = both[:, :, 0].reshape(kv_here * BLOCK, head_dim)
        values = both[:, :, 1].reshape(kv_here * BLOCK, head_dim)
        s = score(q, keys)
        row, col = row_of(kv_here * BLOCK), col_of(kv_here * BLOCK)
        mine = lax.div(lax.rem(row, heads), group) == lax.div(col, BLOCK)
        s = jnp.where(mine, s, LOW)
        before = top_s[p]
        top = jnp.maximum(before, jnp.max(s, 1, keepdims=True))
        s = jnp.exp(s - top[:, :1])
        scale = jnp.exp(before - top)
        total = sum_s[p] * scale + jnp.sum(s, 1, keepdims=True)
        acc = acc_s[p] * scale + jnp.dot(s.astype(jnp.bfloat16), values, preferred_element_type=jnp.float32)
        att[pl.ds(p * steps_heads, steps_heads), :] = acc / total
        return carry

    lax.fori_loop(0, problems, fork_part, 0)

    pairs = heads // 2
    empty = jnp.zeros((rows, head_dim), jnp.bfloat16)
    for i in range(pairs):
        a = att[pl.ds(2 * i, rows, stride=heads), :].astype(jnp.bfloat16)
        b = att[pl.ds(2 * i + 1, rows, stride=heads), :].astype(jnp.bfloat16)
        lhs[0, i] = jnp.concatenate(
            [jnp.concatenate([a, empty], 1), jnp.concatenate([empty, b], 1)], 0
        )

    swap = pltpu.make_async_remote_copy(
        src_ref=lhs.at[0], dst_ref=lhs.at[1], send_sem=swap_sem.at[0], recv_sem=swap_sem.at[1],
        device_id={"cand": sibling}, device_id_type=MESH,
    )
    swap.start()
    for i in range(pieces):
        weight_copy(i).wait()
    swap.wait_recv()

    tiles = parts.shape[1]
    here_tiles = tiles // 2
    per = tile // head_dim

    def part_copy(t, k):
        at = core * here_tiles + t
        return pltpu.make_async_remote_copy(
            src_ref=parts.at[tp_me, at], dst_ref=parts.at[tp_me, at], send_sem=part_send.at[k - 1, t],
            recv_sem=part_recv.at[tp_me, at], device_id={"tp": lax.rem(tp_me + k, tp_n)},
            device_id_type=MESH,
        )

    def other_copy(t, k):
        at = core * here_tiles + t
        return pltpu.make_async_remote_copy(
            src_ref=other.at[t], dst_ref=parts.at[tp_me, at], send_sem=other_send.at[k, t],
            recv_sem=part_recv.at[tp_me, at],
            device_id={"cand": sibling, "tp": lax.rem(tp_me + k, tp_n)}, device_id_type=MESH,
        )

    def project(t, carry):
        at = pl.ds(pl.multiple_of(t * tile, tile), tile)
        first_scale = (core * here_tiles + t) * per
        total = [jnp.zeros((2, rows, head_dim), jnp.float32) for _ in range(per)]
        for i in range(pairs):
            product = jnp.dot(
                lhs[:, i].reshape(4 * rows, 2 * head_dim),
                weights[pl.ds(2 * i * head_dim, 2 * head_dim), at], preferred_element_type=jnp.float32,
            )
            for c in range(per):
                here = product[:, c * head_dim:(c + 1) * head_dim].reshape(2, 2, rows, head_dim)
                total[c] = (
                    total[c] + here[:, 0] * scales[2 * i, first_scale + c]
                    + here[:, 1] * scales[2 * i + 1, first_scale + c]
                )
        whole = jnp.concatenate(total, 2).astype(jnp.bfloat16)
        parts[tp_me, core * here_tiles + t] = whole[0]
        other[t] = whole[1]
        for k in range(1, tp_n):
            other_copy(t, k).start()
            part_copy(t, k).start()
        other_copy(t, 0).start()
        return carry

    lax.fori_loop(0, here_tiles, project, 0)

    def gather(t, carry):
        at = pl.ds(pl.multiple_of(t * tile, tile), tile)

        def arrived(source):
            pltpu.make_async_remote_copy(
                src_ref=other.at[0], dst_ref=parts.at[source, t], send_sem=swap_sem.at[0],
                recv_sem=part_recv.at[source, t], device_id={"cand": sibling}, device_id_type=MESH,
            ).wait_recv()

        @pl.when(lax.div(t, here_tiles) != core)
        def _():
            arrived(tp_me)

        for k in range(1, tp_n):
            arrived(lax.rem(tp_me + k, tp_n))
        total = parts[0, t].astype(jnp.float32)
        for k in range(1, tp_n):
            total = total + parts[k, t].astype(jnp.float32)
        for p in range(problems):
            mixed = hidden[p, :, at].astype(jnp.float32) + total[p * steps:(p + 1) * steps]
            out[p, :, at] = mixed.astype(jnp.bfloat16)
        return carry

    lax.fori_loop(0, tiles, gather, 0)
    swap.wait_send()

    def rest(j):
        sibling_copy(j).wait_send()
        drain0(j)
        drain1(j)
        fork_copy(j).wait_send()

    loop(rest, chunks)

    def rest_parts(t, carry):
        other_copy(t, 0).wait_send()
        for k in range(1, tp_n):
            part_copy(t, k).wait_send()
            other_copy(t, k).wait_send()
        return carry

    lax.fori_loop(0, here_tiles, rest_parts, 0)


def local(cand_n, tp_n, hidden_in, queries, new_kv, kv_cache, lengths, winner, out_values, out_scales):
    problems, kv_here, _, slots, head_dim = kv_cache.shape
    steps, heads = queries.shape[1:3]
    depth, width = out_values.shape
    rows = problems * steps
    split = 4 if kv_here % 4 == 0 else 1
    chunks = problems // 2 * split
    tile = 512
    tiles = width // tile
    flat = queries.reshape(problems, steps * heads, head_dim)
    fresh = jnp.transpose(new_kv, (0, 3, 2, 1, 4))
    fresh = fresh.reshape(problems, 2, kv_here * steps, head_dim)
    smem = pl.BlockSpec(memory_space=pltpu.SMEM)
    vmem = pl.BlockSpec(memory_space=pltpu.VMEM)
    hbm = pl.BlockSpec(memory_space=pl.ANY)
    line = pltpu.VMEM((chunks, kv_here // split, 2, BLOCK, head_dim), jnp.bfloat16)
    stat = pltpu.VMEM((problems, steps * heads, head_dim), jnp.float32)
    dma = pltpu.SemaphoreType.DMA
    blocks = pl.pallas_call(
        pick_kernel,
        out_shape=jax.ShapeDtypeStruct((problems * split, kv_here // split, 2, BLOCK, head_dim), jnp.bfloat16),
        in_specs=[smem, smem, hbm],
        out_specs=vmem,
        scratch_shapes=[
            pltpu.VMEM((problems, kv_here, 2, WINDOW, head_dim), jnp.bfloat16), dma((problems,)),
        ],
        compiler_params=pltpu.CompilerParams(vmem_limit_bytes=67043328 - (2 << 20)),
    )(lengths, winner, kv_cache)
    return pl.pallas_call(
        functools.partial(kernel, cand_n, tp_n, tile, split),
        out_shape=jax.ShapeDtypeStruct(hidden_in.shape, jnp.bfloat16),
        in_specs=[smem, smem, vmem, vmem, vmem, vmem, hbm, hbm],
        out_specs=vmem,
        scratch_shapes=[
            pltpu.VMEM(kv_cache.shape, jnp.bfloat16),
            pltpu.VMEM((depth, width // 2), jnp.bfloat16),
            *[line] * 11,
            pltpu.VMEM((problems * split, kv_here // split, 2, BLOCK, head_dim), jnp.bfloat16),
            stat, stat, stat,
            pltpu.VMEM((problems * steps * heads, head_dim), jnp.float32),
            pltpu.VMEM((2, heads // 2, 2 * rows, 2 * head_dim), jnp.bfloat16),
            pltpu.VMEM((tp_n, tiles, rows, tile), jnp.bfloat16),
            pltpu.VMEM((tiles // 2, rows, tile), jnp.bfloat16),
            dma((problems,)), dma((8,)), dma((8, chunks)), dma((8, chunks)),
            dma((max(tp_n - 1, 1), tiles // 2)), dma((tp_n, tiles)),
            dma((2,)), dma((tp_n, tiles // 2)),
        ],
        compiler_params=pltpu.CompilerParams(
            collective_id=0, has_side_effects=True, vmem_limit_bytes=67043328 - (2 << 20)
        ),
    )(lengths, out_scales, blocks, flat, fresh, hidden_in, kv_cache, out_values)


def solution(mesh):
    placed = (
        P("cand", None, None),
        P("cand", None, "tp", None),
        P("cand", None, "tp", None, None),
        P("cand", "tp", None, None, None),
        P("cand"),
        P(),
        P("tp", None),
        P("tp", None),
    )
    return jax.shard_map(
        functools.partial(local, mesh.shape["cand"], mesh.shape["tp"]),
        mesh=mesh, in_specs=placed, out_specs=P("cand", None, None), check_vma=False,
    )
```

profile of v0, /device:TPU:0, one launch (start us, length us, event | category | flops | bytes accessed | tf_op | source)
XLA Modules:
  0.0 54.3 jit_solution(3751876992881113395)
XLA Ops:
  0.0 1.4 %copy.9 = bf16[8,2,4,2,128]{4,3,2,1,0:T(2,128)(2,1)} copy(bf16[8,2,4,2,128]{4,1,2,3,0:T(2,128)(2,1)} %bitcast.5) | data formatting | bytes 65536 | tf_op jit(solution)/shard_map/transpose | solution.py:419
  1.4 4.3 %shard_map.82.blocks = bf16[32,1,2,64,128]{4,3,2,1,0:T(8,128)(2,1)} custom-call(s32[8]{0:T(128)} %lengths.3, s32[8]{0:T(128)} %winner.1, bf16[8,4,2,512,128]{4,3,2,1,0:T(8,128)(2,1)} %cache_hbm.3), custom_call_target="tpu_custom_call" | custom-call | tf_op jit(solution)/shard_map/pallas_call | solution.py:427
  5.8 46.7 %shard_map.83 = bf16[8,2,8192]{2,1,0:T(2,128)(2,1)} custom-call(s32[8]{0:T(128)} %lengths.3, f32[16,64]{1,0:T(8,128)} %scales.1, bf16[32,1,2,64,128]{4,3,2,1,0:T(8,128)(2,1)} %shard_map.82.blocks, bf16[8,32,128]{2,1,0:T(8,128)(2,1)} %bitcast.4, bf16[8,2,8,128]{3,2,1,0:T(8,128)(2,1)} %bitcast.3, bf16[8,2,8192]{2,1,0:T(2,128)(2,1)} %hidden.1, ...), custom_call_target="tpu_custom_call" | custom-call | tf_op jit(solution)/shard_map/pallas_call | solution.py:437
  52.4 1.8 %copy.11 = bf16[8,2,8192]{2,1,0:T(2,128)(2,1)} copy(bf16[8,2,8192]{2,1,0:T(2,128)(2,1)} %shard_map.83) | data formatting | bytes 524288
where the time goes:
time: 54.5 us; the launch traced here: 54.3 us
  Pallas kernels  51 us (94%)
  local copies, waits for them, and re-layouts  3.23 us (6%)
    pallas_call x1, Pallas kernels, local(): pl.pallas_call(functools.partial(kernel, cand_n, tp_n, tile, split), out_...  46.7 us
    pallas_call x1, Pallas kernels, local(): pl.pallas_call(pick_kernel, out_shape=jax.ShapeDtypeStruct((problems * sp...  4.35 us
    unnamed x1, local copies, waits for them, and re-layouts  1.83 us
    transpose x1, local copies, waits for them, and re-layouts, local(): fresh = jnp.transpose(new_kv, (0, 3, 2, 1, 4))  1.4 us

commit v1 on v0

v1 whole, which is shorter than its diff:
```python
import functools
import math

import jax
import jax.numpy as jnp
from jax import lax
from jax.experimental import pallas as pl
from jax.experimental.pallas import tpu as pltpu
from jax.sharding import PartitionSpec as P

BLOCK = 64
LAG_IN = 4
LAG_OUT = 9
PAIR = 2
LOW = -1e30
MESH = pl.DeviceIdType.MESH


def kernel(
    cand_n, tp_n, tile, split,
    lengths, winner, scales, queries_hbm, fresh_hbm, hidden_hbm, cache_hbm, weights_hbm, out_hbm,
    caches, weights, queries, fresh, hidden, out, blocks, got, own,
    near0, up0, far0, down0, mid, near1, up1, far1, down1,
    fork, top_s, sum_s, acc_s, att, lhs, parts, other,
    cache_sem, weight_sem, small_sem, out_sem, send_sem, recv_sem,
    part_send, part_recv, swap_send, swap_recv, other_send,
):
    me = lax.axis_index("cand")
    tp_me = lax.axis_index("tp")
    problems = len(caches)
    kv_here, _, slots, head_dim = caches[0].shape
    steps_heads = queries.shape[1]
    heads = weights.shape[0] // head_dim
    steps = steps_heads // heads
    group = heads // kv_here
    groups = problems // PAIR
    rows = PAIR * steps
    chunks = groups * split
    core = lax.rem(me, 2)
    chip = lax.div(me, 2)
    outer_len = 4
    inner_len = cand_n // 2 // outer_len
    inner_at = lax.rem(chip, inner_len)
    outer_at = lax.div(chip, inner_len)
    sibling = me + 1 - 2 * core

    def ends(at, length, stride):
        low_side = at < length // 2
        step = jnp.where(low_side, stride, -stride)
        has_near = jnp.logical_and(at > 0, at < length - 1)
        crosses = jnp.logical_or(at == length // 2 - 1, at == length // 2)
        return length, has_near, crosses, me + step, me - step

    inner = ends(inner_at, inner_len, 2)
    outer = ends(outer_at, outer_len, 2 * inner_len)

    pieces = weight_sem.shape[0]
    piece = weights.shape[0] // pieces

    def cache_copy(p):
        return pltpu.make_async_copy(cache_hbm.at[p], caches[p], cache_sem.at[p])

    def weight_copy(i):
        at = pl.ds(i * piece, piece)
        columns = pl.ds(pl.multiple_of(core * weights.shape[1], tile), weights.shape[1])
        return pltpu.make_async_copy(weights_hbm.at[at, columns], weights.at[at], weight_sem.at[i])

    queries_copy = pltpu.make_async_copy(queries_hbm, queries, small_sem.at[0])
    fresh_copy = pltpu.make_async_copy(fresh_hbm, fresh, small_sem.at[1])
    hidden_copy = pltpu.make_async_copy(hidden_hbm, hidden, small_sem.at[2])

    for p in range(PAIR):
        cache_copy(p).start()
    queries_copy.start()
    fresh_copy.start()
    for p in range(PAIR, problems):
        cache_copy(p).start()

    barrier = pltpu.get_barrier_semaphore()

    def greet(**where):
        pl.semaphore_signal(barrier, inc=1, device_id=where, device_id_type=MESH)

    greet(cand=sibling)
    count = 1 + 2 * (tp_n - 1)
    for _, has_near, _, far, near in (inner, outer):
        greet(cand=far)

        @pl.when(has_near)
        def _(near=near):
            greet(cand=near)

        count = count + 1 + has_near.astype(jnp.int32)
    for k in range(1, tp_n):
        greet(tp=lax.rem(tp_me + k, tp_n))
        greet(cand=sibling, tp=lax.rem(tp_me + k, tp_n))

    def remote(src, dst, kind, j, target):
        return pltpu.make_async_remote_copy(
            src_ref=src, dst_ref=dst, send_sem=send_sem.at[kind, j],
            recv_sem=recv_sem.at[kind, j], device_id={"cand": target}, device_id_type=MESH,
        )

    def place(side, j):
        return (PAIR * lax.div(j, split) + side) * split + lax.rem(j, split)

    def sibling_copy(j):
        return remote(blocks.at[place(1 - core, j)], got.at[j], 0, j, sibling)

    def loop(body, first, last):
        def step(j, carry):
            body(j)
            return carry

        lax.fori_loop(first, last, step, 0)

    def make_line(line, kind, base_ref, near_ref, up_ref, far_ref, down_ref):
        length, has_near, crosses, far_id, near_id = line
        short = length == 2
        if short:
            up_ref = base_ref

        def to_far_in(j):
            return remote(up_ref.at[j], near_ref.at[j], kind, j, far_id)

        def to_far_cross(j):
            return remote(up_ref.at[j], far_ref.at[j], kind + 1, j, far_id)

        def to_near(j):
            return pltpu.make_async_remote_copy(
                src_ref=down_ref.at[j], dst_ref=far_ref.at[j], send_sem=send_sem.at[kind + 2, j],
                recv_sem=recv_sem.at[kind + 1, j], device_id={"cand": near_id}, device_id_type=MESH,
            )

        def climb(j):
            if short:
                to_far_cross(j).start()
                return

            @pl.when(has_near)
            def _():
                to_far_in(j).wait_recv()
                up_ref[j] = base_ref[j] + near_ref[j]

            @pl.when(jnp.logical_not(has_near))
            def _():
                up_ref[j] = base_ref[j]

            @pl.when(crosses)
            def _():
                to_far_cross(j).start()

            @pl.when(jnp.logical_not(crosses))
            def _():
                to_far_in(j).start()

        def settle(j):
            to_far_cross(j).wait_recv()
            if not short:
                @pl.when(has_near)
                def _():
                    down_ref[j] = base_ref[j] + far_ref[j]
                    to_near(j).start()

            return up_ref[j] + far_ref[j]

        def drain(j):
            if short:
                to_far_cross(j).wait_send()
                return

            @pl.when(crosses)
            def _():
                to_far_cross(j).wait_send()

            @pl.when(jnp.logical_not(crosses))
            def _():
                to_far_in(j).wait_send()

            @pl.when(has_near)
            def _():
                to_near(j).wait_send()

        return climb, settle, drain

    climb0, settle0, drain0 = make_line(inner, 1, own, near0, up0, far0, down0)
    climb1, settle1, drain1 = make_line(outer, 4, mid, near1, up1, far1, down1)

    def enter(j):
        sibling_copy(j).wait_recv()
        own[j] = blocks[place(core, j)] + got[j]
        climb0(j)

    factor = 1.0 / math.sqrt(head_dim)

    def row_of(width):
        return lax.broadcasted_iota(jnp.int32, (steps_heads, width), 0)

    def col_of(width):
        return lax.broadcasted_iota(jnp.int32, (steps_heads, width), 1)

    def score(q, keys):
        return lax.dot_general(q, keys, (((1,), (1,)), ((), ())), preferred_element_type=jnp.float32) * factor

    pick_row = lax.broadcasted_iota(jnp.int32, (BLOCK, slots), 0)
    pick_col = lax.broadcasted_iota(jnp.int32, (BLOCK, slots), 1)
    hs = kv_here // split

    def pick(p):
        hit = jnp.logical_and(
            pick_col - pick_row == lengths[p] - BLOCK, jnp.zeros_like(pick_col) + winner[p] == me
        )
        chosen = hit.astype(jnp.float32).astype(jnp.bfloat16)
        for h in range(kv_here):
            for kv in range(2):
                blocks[p * split + h // hs, h % hs, kv] = jnp.dot(
                    chosen, caches[p][h, kv], preferred_element_type=jnp.float32
                ).astype(jnp.bfloat16)

    def local_part(p):
        q = queries[p]
        s = score(q, caches[p][:, 0].reshape(kv_here * slots, head_dim))
        row, col = row_of(kv_here * slots), col_of(kv_here * slots)
        mine = lax.div(lax.rem(row, heads), group) == lax.div(col, slots)
        s = jnp.where(jnp.logical_and(mine, lax.rem(col, slots) < lengths[p] - BLOCK), s, LOW)
        both = fresh[p]
        n = score(q, both)
        width = both.shape[0]
        row, col = row_of(width), col_of(width)
        mine = lax.div(lax.rem(row, heads), group) == lax.rem(lax.div(col, 2), kv_here)
        mine = jnp.logical_and(mine, lax.rem(col, 2) == 0)
        n = jnp.where(jnp.logical_and(mine, lax.div(col, 2 * kv_here) <= lax.div(row, heads)), n, LOW)
        wide = both.astype(jnp.float32)
        values = jnp.concatenate([wide[1:], wide[:1]], 0).astype(jnp.bfloat16)
        top = jnp.maximum(jnp.max(s, 1, keepdims=True), jnp.max(n, 1, keepdims=True))
        s = jnp.exp(s - top)
        n = jnp.exp(n - top)
        top_s[p] = jnp.broadcast_to(top, (steps_heads, head_dim))
        sum_s[p] = jnp.broadcast_to(jnp.sum(s, 1, keepdims=True) + jnp.sum(n, 1, keepdims=True), (steps_heads, head_dim))
        acc_s[p] = jnp.dot(
            s.astype(jnp.bfloat16), caches[p][:, 1].reshape(kv_here * slots, head_dim),
            preferred_element_type=jnp.float32,
        ) + jnp.dot(n.astype(jnp.bfloat16), values, preferred_element_type=jnp.float32)

    for g in range(groups):
        for p in range(PAIR * g, PAIR * (g + 1)):
            cache_copy(p).wait()
            pick(p)
        if g == 0:
            pl.semaphore_wait(barrier, count)
        loop(lambda j: sibling_copy(j).start(), g * split, (g + 1) * split)
        if g > 0:
            loop(enter, (g - 1) * split, g * split)
        else:
            queries_copy.wait()
            fresh_copy.wait()
        if g == groups - 1:
            for i in range(pieces):
                weight_copy(i).start()
            hidden_copy.start()
        for p in range(PAIR * g, PAIR * (g + 1)):
            local_part(p)
    loop(enter, (groups - 1) * split, chunks)

    def turn(j):
        mid[j] = settle0(j)
        climb1(j)

    def fork_copy(j):
        at = place(core, j)
        return remote(fork.at[at], fork.at[at], 7, j, sibling)

    def finish(j):
        fork[place(core, j)] = settle1(j)
        fork_copy(j).start()

    def closing(j):
        remote(got.at[j], fork.at[place(1 - core, j)], 7, j, sibling).wait_recv()

    def fork_part(p, slot):
        q = queries[p]
        both = fork[pl.ds(p * split, split)]
        keys = both[:, :, 0].reshape(kv_here * BLOCK, head_dim)
        values = both[:, :, 1].reshape(kv_here * BLOCK, head_dim)
        s = score(q, keys)
        row, col = row_of(kv_here * BLOCK), col_of(kv_here * BLOCK)
        mine = lax.div(lax.rem(row, heads), group) == lax.div(col, BLOCK)
        s = jnp.where(mine, s, LOW)
        before = top_s[p]
        top = jnp.maximum(before, jnp.max(s, 1, keepdims=True))
        s = jnp.exp(s - top[:, :1])
        scale = jnp.exp(before - top)
        total = sum_s[p] * scale + jnp.sum(s, 1, keepdims=True)
        acc = acc_s[p] * scale + jnp.dot(s.astype(jnp.bfloat16), values, preferred_element_type=jnp.float32)
        att[pl.ds(slot * steps_heads, steps_heads), :] = acc / total

    pairs = heads // 2

    def swap_copy(g):
        return pltpu.make_async_remote_copy(
            src_ref=lhs.at[0, g], dst_ref=lhs.at[1, g], send_sem=swap_send.at[g], recv_sem=swap_recv.at[g],
            device_id={"cand": sibling}, device_id_type=MESH,
        )

    def fork_group(g):
        loop(closing, g * split, (g + 1) * split)
        for i in range(PAIR):
            fork_part(PAIR * g + i, i)
        empty = jnp.zeros((rows, head_dim), jnp.float32)
        for i in range(pairs):
            a = att[pl.ds(2 * i, rows, stride=heads), :]
            b = att[pl.ds(2 * i + 1, rows, stride=heads), :]
            lhs[0, g, i] = jnp.concatenate(
                [jnp.concatenate([a, empty], 1), jnp.concatenate([empty, b], 1)], 0
            ).astype(jnp.bfloat16)
        swap_copy(g).start()

    tiles = parts.shape[2]
    here_tiles = tiles // 2
    per = tile // head_dim

    def part_copy(g, t, k):
        at = core * here_tiles + t
        return pltpu.make_async_remote_copy(
            src_ref=parts.at[tp_me, g, at], dst_ref=parts.at[tp_me, g, at], send_sem=part_send.at[k - 1, g, t],
            recv_sem=part_recv.at[tp_me, g, at], device_id={"tp": lax.rem(tp_me + k, tp_n)},
            device_id_type=MESH,
        )

    def other_copy(g, t, k):
        at = core * here_tiles + t
        return pltpu.make_async_remote_copy(
            src_ref=other.at[g, t], dst_ref=parts.at[tp_me, g, at], send_sem=other_send.at[k, g, t],
            recv_sem=part_recv.at[tp_me, g, at],
            device_id={"cand": sibling, "tp": lax.rem(tp_me + k, tp_n)}, device_id_type=MESH,
        )

    def project(g, t):
        at = pl.ds(pl.multiple_of(t * tile, tile), tile)
        first_scale = (core * here_tiles + t) * per
        row = lax.broadcasted_iota(jnp.int32, (4 * rows, head_dim), 0)
        even = lax.rem(row, 2 * rows) < rows
        total = [jnp.zeros((4 * rows, head_dim), jnp.float32) for _ in range(per)]
        for i in range(pairs):
            product = jnp.dot(
                lhs[:, g, i].reshape(4 * rows, 2 * head_dim),
                weights[pl.ds(2 * i * head_dim, 2 * head_dim), at], preferred_element_type=jnp.float32,
            )
            for c in range(per):
                scale = jnp.where(even, scales[2 * i, first_scale + c], scales[2 * i + 1, first_scale + c])
                total[c] = total[c] + product[:, c * head_dim:(c + 1) * head_dim] * scale
        whole = jnp.concatenate(total, 1).reshape(2, 2, rows, tile)
        whole = (whole[:, 0] + whole[:, 1]).astype(jnp.bfloat16)
        parts[tp_me, g, core * here_tiles + t] = whole[0]
        other[g, t] = whole[1]
        for k in range(1, tp_n):
            other_copy(g, t, k).start()
            part_copy(g, t, k).start()
        other_copy(g, t, 0).start()

    share = here_tiles // split

    def project_piece(g, at):
        @pl.when(at == 0)
        def _():
            @pl.when(g == 0)
            def _():
                for i in range(pieces):
                    weight_copy(i).wait()

            swap_copy(g).wait_recv()

        loop(lambda t: project(g, t), at * share, (at + 1) * share)

    def out_copy(g):
        at = pl.ds(PAIR * g, PAIR)
        return pltpu.make_async_copy(out.at[at], out_hbm.at[at], out_sem.at[g])

    def gather_tile(g, t):
        at = pl.ds(pl.multiple_of(t * tile, tile), tile)

        def arrived(source):
            pltpu.make_async_remote_copy(
                src_ref=other.at[0, 0], dst_ref=parts.at[source, g, t], send_sem=swap_send.at[0],
                recv_sem=part_recv.at[source, g, t], device_id={"cand": sibling}, device_id_type=MESH,
            ).wait_recv()

        @pl.when(lax.div(t, here_tiles) != core)
        def _():
            arrived(tp_me)

        for k in range(1, tp_n):
            arrived(lax.rem(tp_me + k, tp_n))
        total = parts[0, g, t].astype(jnp.float32)
        for k in range(1, tp_n):
            total = total + parts[k, g, t].astype(jnp.float32)
        for i in range(PAIR):
            mixed = hidden[PAIR * g + i, :, at].astype(jnp.float32) + total[i * steps:(i + 1) * steps]
            out[PAIR * g + i, :, at] = mixed.astype(jnp.bfloat16)

    def gather(g):
        @pl.when(g == 0)
        def _():
            hidden_copy.wait()

        def both_halves(t):
            gather_tile(g, t)
            gather_tile(g, t + here_tiles)

        loop(both_halves, 0, here_tiles)
        out_copy(g).start()

    fork_at = split + 1
    project_at = fork_at + 2
    gather_at = project_at + split + 3

    def within(at, length):
        return jnp.logical_and(at >= 0, at < length)

    def advance(i):
        @pl.when(i < chunks)
        def _():
            turn(i)

        @pl.when(jnp.logical_and(outer[1], within(i - LAG_IN, chunks)))
        def _():
            finish(i - LAG_IN)

        now = i - LAG_OUT

        @pl.when(jnp.logical_and(jnp.logical_not(outer[1]), within(now, chunks)))
        def _():
            finish(now)

        def starts(at):
            return jnp.logical_and(within(now - at, chunks), lax.rem(now - at + chunks, split) == 0)

        @pl.when(starts(fork_at))
        def _():
            fork_group(lax.div(now - fork_at, split))

        @pl.when(within(now - project_at, chunks))
        def _():
            at = now - project_at
            project_piece(lax.div(at, split), lax.rem(at, split))

        @pl.when(starts(gather_at))
        def _():
            gather(lax.div(now - gather_at, split))

    loop(advance, 0, LAG_OUT + gather_at + chunks)

    def rest(j):
        sibling_copy(j).wait_send()
        drain0(j)
        drain1(j)
        fork_copy(j).wait_send()

    loop(rest, 0, chunks)

    def rest_group(g):
        swap_copy(g).wait_send()

        def rest_parts(t):
            other_copy(g, t, 0).wait_send()
            for k in range(1, tp_n):
                part_copy(g, t, k).wait_send()
                other_copy(g, t, k).wait_send()

        loop(rest_parts, 0, here_tiles)
        out_copy(g).wait()

    loop(rest_group, 0, groups)


def local(cand_n, tp_n, hidden_in, queries, new_kv, kv_cache, lengths, winner, out_values, out_scales):
    problems, kv_here, _, slots, head_dim = kv_cache.shape
    steps, heads = queries.shape[1:3]
    depth, width = out_values.shape
    groups = problems // PAIR
    rows = PAIR * steps
    split = 4 if kv_here % 4 == 0 else 1
    hs = kv_here // split
    chunks = groups * split
    tile = 512
    tiles = width // tile
    flat = queries.reshape(problems, steps * heads, head_dim)
    fresh = new_kv.reshape(problems, steps * kv_here * 2, head_dim)
    smem = pl.BlockSpec(memory_space=pltpu.SMEM)
    hbm = pl.BlockSpec(memory_space=pl.ANY)
    line = pltpu.VMEM((chunks, hs, 2, BLOCK, head_dim), jnp.bfloat16)
    none = pltpu.VMEM((1, hs, 2, BLOCK, head_dim), jnp.bfloat16)
    short = cand_n // 2 // 4 == 2
    spare = none if short else line
    every = pltpu.VMEM((problems * split, hs, 2, BLOCK, head_dim), jnp.bfloat16)
    stat = pltpu.VMEM((problems, steps * heads, head_dim), jnp.float32)
    dma = pltpu.SemaphoreType.DMA
    return pl.pallas_call(
        functools.partial(kernel, cand_n, tp_n, tile, split),
        out_shape=jax.ShapeDtypeStruct(hidden_in.shape, jnp.bfloat16),
        in_specs=[smem, smem, smem, hbm, hbm, hbm, hbm, hbm],
        out_specs=hbm,
        scratch_shapes=[
            [pltpu.VMEM(kv_cache.shape[1:], jnp.bfloat16)] * problems,
            pltpu.VMEM((depth, width // 2), jnp.bfloat16),
            pltpu.VMEM(flat.shape, jnp.bfloat16),
            pltpu.VMEM(fresh.shape, jnp.bfloat16),
            pltpu.VMEM(hidden_in.shape, jnp.bfloat16),
            pltpu.VMEM(hidden_in.shape, jnp.bfloat16),
            every, line, line,
            spare, spare, line, spare,
            *[line] * 5,
            every, stat, stat, stat,
            pltpu.VMEM((PAIR * steps * heads, head_dim), jnp.float32),
            pltpu.VMEM((2, groups, heads // 2, 2 * rows, 2 * head_dim), jnp.bfloat16),
            pltpu.VMEM((tp_n, groups, tiles, rows, tile), jnp.bfloat16),
            pltpu.VMEM((groups, tiles // 2, rows, tile), jnp.bfloat16),
            dma((problems,)), dma((8,)), dma((3,)), dma((groups,)), dma((8, chunks)), dma((8, chunks)),
            dma((max(tp_n - 1, 1), groups, tiles // 2)), dma((tp_n, groups, tiles)),
            dma((groups,)), dma((groups,)), dma((tp_n, groups, tiles // 2)),
        ],
        compiler_params=pltpu.CompilerParams(
            collective_id=0, has_side_effects=True, vmem_limit_bytes=67043328 - (2 << 20)
        ),
    )(lengths, winner, out_scales, flat, fresh, hidden_in, kv_cache, out_values)


def solution(mesh):
    placed = (
        P("cand", None, None),
        P("cand", None, "tp", None),
        P("cand", None, "tp", None, None),
        P("cand", "tp", None, None, None),
        P("cand"),
        P(),
        P("tp", None),
        P("tp", None),
    )
    return jax.shard_map(
        functools.partial(local, mesh.shape["cand"], mesh.shape["tp"]),
        mesh=mesh, in_specs=placed, out_specs=P("cand", None, None), check_vma=False,
    )
```

time: 54.5 us -> 57.2 us (1.050)
  Pallas kernels: 51 us -> 55.1 us
  local copies, waits for them, and re-layouts: 3.23 us -> 1.83 us
    pallas_call x1, Pallas kernels: 46.7 us -> 55.1 us  [local(): pl.pallas_call(functools.partial(kernel, cand_n, tp_n, tile, split), out_...]
    pallas_call x1 -> x0, Pallas kernels: 4.35 us -> none  [local(): pl.pallas_call(pick_kernel, out_shape=jax.ShapeDtypeStruct((problems * sp...]
    transpose x1 -> x0, local copies, waits for them, and re-layouts: 1.4 us -> none  [local(): fresh = jnp.transpose(new_kv, (0, 3, 2, 1, 4))]
where the time goes in v1:
time: 57.2 us; the launch traced here: 57 us
  Pallas kernels  55.1 us (96%)
  local copies, waits for them, and re-layouts  1.83 us (3%)
    pallas_call x1, Pallas kernels, local(): pl.pallas_call(functools.partial(kernel, cand_n, tp_n, tile, split), out_...  55.1 us
    unnamed x1, local copies, waits for them, and re-layouts  1.83 us

profile of v1, /device:TPU:0, one launch (start us, length us, event | category | flops | bytes accessed | tf_op | source)
XLA Modules:
  0.0 57.0 jit_solution(16517934266014996941)
XLA Ops:
  0.0 55.1 %shard_map.82 = bf16[8,2,8192]{2,1,0:T(2,128)(2,1)} custom-call(s32[8]{0:T(128)} %lengths.1, s32[8]{0:T(128)} %winner.1, f32[16,64]{1,0:T(8,128)} %scales.1, bf16[8,32,128]{2,1,0:T(8,128)(2,1)} %bitcast.2, bf16[8,16,128]{2,1,0:T(8,128)(2,1)} %bitcast.3, bf16[8,2,8192]{2,1,0:T(2,128)(2,1)} %hidden_hbm.1, bf16[8,4,2,512,128]{4,3,2,1,0:T(8,128)(2,1)} %cache_hbm.1, ...), custom_call_target="tpu_custom_call" | custom-call | tf_op jit(solution)/shard_map/pallas_call | solution.py:498
  55.1 1.8 %copy.10 = bf16[8,2,8192]{2,1,0:T(2,128)(2,1)} copy(bf16[8,2,8192]{2,1,0:T(2,128)(2,1)} %shard_map.82) | data formatting | bytes 524288

commit v2 on v1

--- a/solution.py
+++ b/solution.py
@@ -10,8 +10,9 @@
 
 BLOCK = 64
 LAG_IN = 4
-LAG_OUT = 9
+LAG_OUT = 12
 PAIR = 2
+GROUP = 4
 LOW = -1e30
 MESH = pl.DeviceIdType.MESH
 
@@ -33,9 +34,10 @@
     heads = weights.shape[0] // head_dim
     steps = steps_heads // heads
     group = heads // kv_here
-    groups = problems // PAIR
-    rows = PAIR * steps
-    chunks = groups * split
+    groups = problems // GROUP
+    rows = GROUP * steps
+    chunks = problems // PAIR * split
+    span = GROUP // PAIR * split
     core = lax.rem(me, 2)
     chip = lax.div(me, 2)
     outer_len = 4
@@ -242,7 +244,7 @@
             preferred_element_type=jnp.float32,
         ) + jnp.dot(n.astype(jnp.bfloat16), values, preferred_element_type=jnp.float32)
 
-    for g in range(groups):
+    for g in range(problems // PAIR):
         for p in range(PAIR * g, PAIR * (g + 1)):
             cache_copy(p).wait()
             pick(p)
@@ -251,16 +253,16 @@
         loop(lambda j: sibling_copy(j).start(), g * split, (g + 1) * split)
         if g > 0:
             loop(enter, (g - 1) * split, g * split)
-        else:
-            queries_copy.wait()
-            fresh_copy.wait()
-        if g == groups - 1:
-            for i in range(pieces):
-                weight_copy(i).start()
-            hidden_copy.start()
-        for p in range(PAIR * g, PAIR * (g + 1)):
-            local_part(p)
-    loop(enter, (groups - 1) * split, chunks)
+    for i in range(pieces):
+        weight_copy(i).start()
+    hidden_copy.start()
+    queries_copy.wait()
+    fresh_copy.wait()
+    early = problems // 2
+    local_part(0)
+    loop(enter, chunks - split, chunks)
+    for p in range(1, early):
+        local_part(p)
 
     def turn(j):
         mid[j] = settle0(j)
@@ -303,9 +305,8 @@
         )
 
     def fork_group(g):
-        loop(closing, g * split, (g + 1) * split)
-        for i in range(PAIR):
-            fork_part(PAIR * g + i, i)
+        loop(closing, g * span, (g + 1) * span)
+        loop(lambda i: fork_part(GROUP * g + i, i), 0, GROUP)
         empty = jnp.zeros((rows, head_dim), jnp.float32)
         for i in range(pairs):
             a = att[pl.ds(2 * i, rows, stride=heads), :]
@@ -358,22 +359,21 @@
             part_copy(g, t, k).start()
         other_copy(g, t, 0).start()
 
-    share = here_tiles // split
+    share = max(here_tiles // span, 1)
+    turns = here_tiles // share
 
     def project_piece(g, at):
         @pl.when(at == 0)
         def _():
-            @pl.when(g == 0)
-            def _():
+            if g == 0:
                 for i in range(pieces):
                     weight_copy(i).wait()
-
             swap_copy(g).wait_recv()
 
         loop(lambda t: project(g, t), at * share, (at + 1) * share)
 
     def out_copy(g):
-        at = pl.ds(PAIR * g, PAIR)
+        at = pl.ds(GROUP * g, GROUP)
         return pltpu.make_async_copy(out.at[at], out_hbm.at[at], out_sem.at[g])
 
     def gather_tile(g, t):
@@ -394,13 +394,12 @@
         total = parts[0, g, t].astype(jnp.float32)
         for k in range(1, tp_n):
             total = total + parts[k, g, t].astype(jnp.float32)
-        for i in range(PAIR):
-            mixed = hidden[PAIR * g + i, :, at].astype(jnp.float32) + total[i * steps:(i + 1) * steps]
-            out[PAIR * g + i, :, at] = mixed.astype(jnp.bfloat16)
+        for i in range(GROUP):
+            mixed = hidden[GROUP * g + i, :, at].astype(jnp.float32) + total[i * steps:(i + 1) * steps]
+            out[GROUP * g + i, :, at] = mixed.astype(jnp.bfloat16)
 
     def gather(g):
-        @pl.when(g == 0)
-        def _():
+        if g == 0:
             hidden_copy.wait()
 
         def both_halves(t):
@@ -410,9 +409,9 @@
         loop(both_halves, 0, here_tiles)
         out_copy(g).start()
 
-    fork_at = split + 1
+    fork_at = span + 1
     project_at = fork_at + 2
-    gather_at = project_at + split + 3
+    gather_at = project_at + turns + 3
 
     def within(at, length):
         return jnp.logical_and(at >= 0, at < length)
@@ -422,6 +421,11 @@
         def _():
             turn(i)
 
+        for p in range(early, problems):
+            @pl.when(i == p - early)
+            def _(p=p):
+                local_part(p)
+
         @pl.when(jnp.logical_and(outer[1], within(i - LAG_IN, chunks)))
         def _():
             finish(i - LAG_IN)
@@ -432,23 +436,22 @@
         def _():
             finish(now)
 
-        def starts(at):
-            return jnp.logical_and(within(now - at, chunks), lax.rem(now - at + chunks, split) == 0)
-
-        @pl.when(starts(fork_at))
-        def _():
-            fork_group(lax.div(now - fork_at, split))
-
-        @pl.when(within(now - project_at, chunks))
-        def _():
-            at = now - project_at
-            project_piece(lax.div(at, split), lax.rem(at, split))
-
-        @pl.when(starts(gather_at))
-        def _():
-            gather(lax.div(now - gather_at, split))
-
-    loop(advance, 0, LAG_OUT + gather_at + chunks)
+        for g in range(groups):
+            at = now - g * span
+
+            @pl.when(at == fork_at)
+            def _(g=g):
+                fork_group(g)
+
+            @pl.when(within(at - project_at, turns))
+            def _(g=g, at=at):
+                project_piece(g, at - project_at)
+
+            @pl.when(at == gather_at)
+            def _(g=g):
+                gather(g)
+
+    loop(advance, 0, LAG_OUT + gather_at + (groups - 1) * span + 1)
 
     def rest(j):
         sibling_copy(j).wait_send()
@@ -477,11 +480,11 @@
     problems, kv_here, _, slots, head_dim = kv_cache.shape
     steps, heads = queries.shape[1:3]
     depth, width = out_values.shape
-    groups = problems // PAIR
-    rows = PAIR * steps
+    groups = problems // GROUP
+    rows = GROUP * steps
     split = 4 if kv_here % 4 == 0 else 1
     hs = kv_here // split
-    chunks = groups * split
+    chunks = problems // PAIR * split
     tile = 512
     tiles = width // tile
     flat = queries.reshape(problems, steps * heads, head_dim)
@@ -511,7 +514,7 @@
             spare, spare, line, spare,
             *[line] * 5,
             every, stat, stat, stat,
-            pltpu.VMEM((PAIR * steps * heads, head_dim), jnp.float32),
+            pltpu.VMEM((GROUP * steps * heads, head_dim), jnp.float32),
             pltpu.VMEM((2, groups, heads // 2, 2 * rows, 2 * head_dim), jnp.bfloat16),
             pltpu.VMEM((tp_n, groups, tiles, rows, tile), jnp.bfloat16),
             pltpu.VMEM((groups, tiles // 2, rows, tile), jnp.bfloat16),

time: 57.2 us -> 51 us (0.89)
  Pallas kernels: 55.1 us -> 48.9 us
    pallas_call x1, Pallas kernels: 55.1 us -> 48.9 us  [local(): pl.pallas_call(functools.partial(kernel, cand_n, tp_n, tile, split), out_...]
where the time goes in v2:
time: 51 us; the launch traced here: 50.8 us
  Pallas kernels  48.9 us (96%)
  local copies, waits for them, and re-layouts  1.83 us (4%)
    pallas_call x1, Pallas kernels, local(): pl.pallas_call(functools.partial(kernel, cand_n, tp_n, tile, split), out_...  48.9 us
    unnamed x1, local copies, waits for them, and re-layouts  1.83 us

profile of v2, /device:TPU:0, one launch (start us, length us, event | category | flops | bytes accessed | tf_op | source)
XLA Modules:
  0.0 50.8 jit_solution(6608871523545443695)
XLA Ops:
  0.0 48.9 %shard_map.82 = bf16[8,2,8192]{2,1,0:T(2,128)(2,1)} custom-call(s32[8]{0:T(128)} %lengths.1, s32[8]{0:T(128)} %winner.1, f32[16,64]{1,0:T(8,128)} %scales.1, bf16[8,32,128]{2,1,0:T(8,128)(2,1)} %bitcast.2, bf16[8,16,128]{2,1,0:T(8,128)(2,1)} %bitcast.3, bf16[8,2,8192]{2,1,0:T(2,128)(2,1)} %hidden_hbm.1, bf16[8,4,2,512,128]{4,3,2,1,0:T(8,128)(2,1)} %cache_hbm.1, ...), custom_call_target="tpu_custom_call" | custom-call | tf_op jit(solution)/shard_map/pallas_call | solution.py:501
  48.9 1.8 %copy.10 = bf16[8,2,8192]{2,1,0:T(2,128)(2,1)} copy(bf16[8,2,8192]{2,1,0:T(2,128)(2,1)} %shard_map.82) | data formatting | bytes 524288

commit v3 on v2

--- a/solution.py
+++ b/solution.py
@@ -9,10 +9,11 @@
 from jax.sharding import PartitionSpec as P
 
 BLOCK = 64
-LAG_IN = 4
-LAG_OUT = 12
+LAG_IN = 3
+LAG_OUT = 8
 PAIR = 2
 GROUP = 4
+UNIT = 4
 LOW = -1e30
 MESH = pl.DeviceIdType.MESH
 
@@ -31,7 +32,8 @@
     problems = len(caches)
     kv_here, _, slots, head_dim = caches[0].shape
     steps_heads = queries.shape[1]
-    heads = weights.shape[0] // head_dim
+    strips, depth, lanes = weights.shape
+    heads = depth // head_dim
     steps = steps_heads // heads
     group = heads // kv_here
     groups = problems // GROUP
@@ -56,16 +58,12 @@
     inner = ends(inner_at, inner_len, 2)
     outer = ends(outer_at, outer_len, 2 * inner_len)
 
-    pieces = weight_sem.shape[0]
-    piece = weights.shape[0] // pieces
-
     def cache_copy(p):
         return pltpu.make_async_copy(cache_hbm.at[p], caches[p], cache_sem.at[p])
 
     def weight_copy(i):
-        at = pl.ds(i * piece, piece)
-        columns = pl.ds(pl.multiple_of(core * weights.shape[1], tile), weights.shape[1])
-        return pltpu.make_async_copy(weights_hbm.at[at, columns], weights.at[at], weight_sem.at[i])
+        columns = pl.ds(pl.multiple_of((core * strips + i) * lanes, lanes), lanes)
+        return pltpu.make_async_copy(weights_hbm.at[:, columns], weights.at[i], weight_sem.at[i])
 
     queries_copy = pltpu.make_async_copy(queries_hbm, queries, small_sem.at[0])
     fresh_copy = pltpu.make_async_copy(fresh_hbm, fresh, small_sem.at[1])
@@ -206,7 +204,7 @@
 
     pick_row = lax.broadcasted_iota(jnp.int32, (BLOCK, slots), 0)
     pick_col = lax.broadcasted_iota(jnp.int32, (BLOCK, slots), 1)
-    hs = kv_here // split
+    unit = blocks.shape[1]
 
     def pick(p):
         hit = jnp.logical_and(
@@ -215,7 +213,8 @@
         chosen = hit.astype(jnp.float32).astype(jnp.bfloat16)
         for h in range(kv_here):
             for kv in range(2):
-                blocks[p * split + h // hs, h % hs, kv] = jnp.dot(
+                at = p * kv_here * 2 + h * 2 + kv
+                blocks[at // unit, at % unit] = jnp.dot(
                     chosen, caches[p][h, kv], preferred_element_type=jnp.float32
                 ).astype(jnp.bfloat16)
 
@@ -253,8 +252,7 @@
         loop(lambda j: sibling_copy(j).start(), g * split, (g + 1) * split)
         if g > 0:
             loop(enter, (g - 1) * split, g * split)
-    for i in range(pieces):
-        weight_copy(i).start()
+    loop(lambda i: weight_copy(i).start(), 0, strips)
     hidden_copy.start()
     queries_copy.wait()
     fresh_copy.wait()
@@ -281,9 +279,9 @@
 
     def fork_part(p, slot):
         q = queries[p]
-        both = fork[pl.ds(p * split, split)]
-        keys = both[:, :, 0].reshape(kv_here * BLOCK, head_dim)
-        values = both[:, :, 1].reshape(kv_here * BLOCK, head_dim)
+        both = fork[pl.ds(p * split, split)].reshape(kv_here, 2, BLOCK, head_dim)
+        keys = both[:, 0].reshape(kv_here * BLOCK, head_dim)
+        values = both[:, 1].reshape(kv_here * BLOCK, head_dim)
         s = score(q, keys)
         row, col = row_of(kv_here * BLOCK), col_of(kv_here * BLOCK)
         mine = lax.div(lax.rem(row, heads), group) == lax.div(col, BLOCK)
@@ -337,15 +335,15 @@
         )
 
     def project(g, t):
-        at = pl.ds(pl.multiple_of(t * tile, tile), tile)
         first_scale = (core * here_tiles + t) * per
         row = lax.broadcasted_iota(jnp.int32, (4 * rows, head_dim), 0)
         even = lax.rem(row, 2 * rows) < rows
         total = [jnp.zeros((4 * rows, head_dim), jnp.float32) for _ in range(per)]
         for i in range(pairs):
+            block = [weights[t * per + c, pl.ds(2 * i * head_dim, 2 * head_dim)] for c in range(per)]
             product = jnp.dot(
-                lhs[:, g, i].reshape(4 * rows, 2 * head_dim),
-                weights[pl.ds(2 * i * head_dim, 2 * head_dim), at], preferred_element_type=jnp.float32,
+                lhs[:, g, i].reshape(4 * rows, 2 * head_dim), jnp.concatenate(block, 1),
+                preferred_element_type=jnp.float32,
             )
             for c in range(per):
                 scale = jnp.where(even, scales[2 * i, first_scale + c], scales[2 * i + 1, first_scale + c])
@@ -365,12 +363,15 @@
     def project_piece(g, at):
         @pl.when(at == 0)
         def _():
+            swap_copy(g).wait_recv()
+
+        def one(t):
             if g == 0:
-                for i in range(pieces):
-                    weight_copy(i).wait()
-            swap_copy(g).wait_recv()
-
-        loop(lambda t: project(g, t), at * share, (at + 1) * share)
+                for c in range(per):
+                    weight_copy(t * per + c).wait()
+            project(g, t)
+
+        loop(one, at * share, (at + 1) * share)
 
     def out_copy(g):
         at = pl.ds(GROUP * g, GROUP)
@@ -409,9 +410,9 @@
         loop(both_halves, 0, here_tiles)
         out_copy(g).start()
 
-    fork_at = span + 1
-    project_at = fork_at + 2
-    gather_at = project_at + turns + 3
+    fork_at = span
+    project_at = fork_at + 1
+    gather_at = project_at + turns
 
     def within(at, length):
         return jnp.logical_and(at >= 0, at < length)
@@ -432,24 +433,28 @@
 
         now = i - LAG_OUT
 
+        for g in range(groups):
+            at = now - g * span
+
+            @pl.when(at == gather_at)
+            def _(g=g):
+                gather(g)
+
+        for g in range(groups):
+            at = now - g * span
+
+            @pl.when(within(at - project_at, turns))
+            def _(g=g, at=at):
+                project_piece(g, at - project_at)
+
+        for g in range(groups):
+            @pl.when(now - g * span == fork_at)
+            def _(g=g):
+                fork_group(g)
+
         @pl.when(jnp.logical_and(jnp.logical_not(outer[1]), within(now, chunks)))
         def _():
             finish(now)
-
-        for g in range(groups):
-            at = now - g * span
-
-            @pl.when(at == fork_at)
-            def _(g=g):
-                fork_group(g)
-
-            @pl.when(within(at - project_at, turns))
-            def _(g=g, at=at):
-                project_piece(g, at - project_at)
-
-            @pl.when(at == gather_at)
-            def _(g=g):
-                gather(g)
 
     loop(advance, 0, LAG_OUT + gather_at + (groups - 1) * span + 1)
 
@@ -482,20 +487,21 @@
     depth, width = out_values.shape
     groups = problems // GROUP
     rows = GROUP * steps
-    split = 4 if kv_here % 4 == 0 else 1
-    hs = kv_here // split
+    unit = min(UNIT, kv_here * 2)
+    split = kv_here * 2 // unit
     chunks = problems // PAIR * split
-    tile = 512
+    tile = 1024
     tiles = width // tile
+    strips = width // 2 // 128
     flat = queries.reshape(problems, steps * heads, head_dim)
     fresh = new_kv.reshape(problems, steps * kv_here * 2, head_dim)
     smem = pl.BlockSpec(memory_space=pltpu.SMEM)
     hbm = pl.BlockSpec(memory_space=pl.ANY)
-    line = pltpu.VMEM((chunks, hs, 2, BLOCK, head_dim), jnp.bfloat16)
-    none = pltpu.VMEM((1, hs, 2, BLOCK, head_dim), jnp.bfloat16)
+    line = pltpu.VMEM((chunks, unit, BLOCK, head_dim), jnp.bfloat16)
+    none = pltpu.VMEM((1, unit, BLOCK, head_dim), jnp.bfloat16)
     short = cand_n // 2 // 4 == 2
     spare = none if short else line
-    every = pltpu.VMEM((problems * split, hs, 2, BLOCK, head_dim), jnp.bfloat16)
+    every = pltpu.VMEM((problems * split, unit, BLOCK, head_dim), jnp.bfloat16)
     stat = pltpu.VMEM((problems, steps * heads, head_dim), jnp.float32)
     dma = pltpu.SemaphoreType.DMA
     return pl.pallas_call(
@@ -505,7 +511,7 @@
         out_specs=hbm,
         scratch_shapes=[
             [pltpu.VMEM(kv_cache.shape[1:], jnp.bfloat16)] * problems,
-            pltpu.VMEM((depth, width // 2), jnp.bfloat16),
+            pltpu.VMEM((strips, depth, 128), jnp.bfloat16),
             pltpu.VMEM(flat.shape, jnp.bfloat16),
             pltpu.VMEM(fresh.shape, jnp.bfloat16),
             pltpu.VMEM(hidden_in.shape, jnp.bfloat16),
@@ -518,7 +524,7 @@
             pltpu.VMEM((2, groups, heads // 2, 2 * rows, 2 * head_dim), jnp.bfloat16),
             pltpu.VMEM((tp_n, groups, tiles, rows, tile), jnp.bfloat16),
             pltpu.VMEM((groups, tiles // 2, rows, tile), jnp.bfloat16),
-            dma((problems,)), dma((8,)), dma((3,)), dma((groups,)), dma((8, chunks)), dma((8, chunks)),
+            dma((problems,)), dma((strips,)), dma((3,)), dma((groups,)), dma((8, chunks)), dma((8, chunks)),
             dma((max(tp_n - 1, 1), groups, tiles // 2)), dma((tp_n, groups, tiles)),
             dma((groups,)), dma((groups,)), dma((tp_n, groups, tiles // 2)),
         ],

time: 51 us -> 48.4 us (0.949)
  Pallas kernels: 48.9 us -> 46.3 us
    pallas_call x1, Pallas kernels: 48.9 us -> 46.3 us  [local(): pl.pallas_call(functools.partial(kernel, cand_n, tp_n, tile, split), out_...]
where the time goes in v3:
time: 48.4 us; the launch traced here: 48.2 us
  Pallas kernels  46.3 us (96%)
  local copies, waits for them, and re-layouts  1.83 us (4%)
    pallas_call x1, Pallas kernels, local(): pl.pallas_call(functools.partial(kernel, cand_n, tp_n, tile, split), out_...  46.3 us
    unnamed x1, local copies, waits for them, and re-layouts  1.83 us

profile of v3, /device:TPU:0, one launch (start us, length us, event | category | flops | bytes accessed | tf_op | source)
XLA Modules:
  0.0 48.2 jit_solution(17074506514575437980)
XLA Ops:
  0.0 46.3 %shard_map.82 = bf16[8,2,8192]{2,1,0:T(2,128)(2,1)} custom-call(s32[8]{0:T(128)} %lengths.1, s32[8]{0:T(128)} %winner.1, f32[16,64]{1,0:T(8,128)} %scales.1, bf16[8,32,128]{2,1,0:T(8,128)(2,1)} %bitcast.2, bf16[8,16,128]{2,1,0:T(8,128)(2,1)} %bitcast.3, bf16[8,2,8192]{2,1,0:T(2,128)(2,1)} %hidden_hbm.1, bf16[8,4,2,512,128]{4,3,2,1,0:T(8,128)(2,1)} %cache_hbm.1, ...), custom_call_target="tpu_custom_call" | custom-call | tf_op jit(solution)/shard_map/pallas_call | solution.py:507
  46.3 1.8 %copy.10 = bf16[8,2,8192]{2,1,0:T(2,128)(2,1)} copy(bf16[8,2,8192]{2,1,0:T(2,128)(2,1)} %shard_map.82) | data formatting | bytes 524288

commit v4 on v3

--- a/solution.py
+++ b/solution.py
@@ -11,6 +11,7 @@
 BLOCK = 64
 LAG_IN = 3
 LAG_OUT = 8
+LAG_X = 3
 PAIR = 2
 GROUP = 4
 UNIT = 4
@@ -53,7 +54,7 @@
         step = jnp.where(low_side, stride, -stride)
         has_near = jnp.logical_and(at > 0, at < length - 1)
         crosses = jnp.logical_or(at == length // 2 - 1, at == length // 2)
-        return length, has_near, crosses, me + step, me - step
+        return has_near, crosses, me + step, me - step
 
     inner = ends(inner_at, inner_len, 2)
     outer = ends(outer_at, outer_len, 2 * inner_len)
@@ -83,7 +84,7 @@
 
     greet(cand=sibling)
     count = 1 + 2 * (tp_n - 1)
-    for _, has_near, _, far, near in (inner, outer):
+    for has_near, _, far, near in (inner, outer):
         greet(cand=far)
 
         @pl.when(has_near)
@@ -115,10 +116,7 @@
         lax.fori_loop(first, last, step, 0)
 
     def make_line(line, kind, base_ref, near_ref, up_ref, far_ref, down_ref):
-        length, has_near, crosses, far_id, near_id = line
-        short = length == 2
-        if short:
-            up_ref = base_ref
+        has_near, crosses, far_id, near_id = line
 
         def to_far_in(j):
             return remote(up_ref.at[j], near_ref.at[j], kind, j, far_id)
@@ -133,10 +131,6 @@
             )
 
         def climb(j):
-            if short:
-                to_far_cross(j).start()
-                return
-
             @pl.when(has_near)
             def _():
                 to_far_in(j).wait_recv()
@@ -156,22 +150,18 @@
 
         def settle(j):
             to_far_cross(j).wait_recv()
-            if not short:
-                @pl.when(has_near)
-                def _():
-                    down_ref[j] = base_ref[j] + far_ref[j]
-                    to_near(j).start()
+
+            @pl.when(has_near)
+            def _():
+                down_ref[j] = base_ref[j] + far_ref[j]
+                to_near(j).start()
 
             return up_ref[j] + far_ref[j]
 
         def drain(j):
-            if short:
+            @pl.when(crosses)
+            def _():
                 to_far_cross(j).wait_send()
-                return
-
-            @pl.when(crosses)
-            def _():
-                to_far_cross(j).wait_send()
 
             @pl.when(jnp.logical_not(crosses))
             def _():
@@ -183,8 +173,17 @@
 
         return climb, settle, drain
 
-    climb0, settle0, drain0 = make_line(inner, 1, own, near0, up0, far0, down0)
-    climb1, settle1, drain1 = make_line(outer, 4, mid, near1, up1, far1, down1)
+    def choose(a, b):
+        return (
+            *[jnp.logical_or(jnp.logical_and(core == 0, p), jnp.logical_and(core == 1, q)) for p, q in zip(a[:2], b[:2])],
+            *[jnp.where(core == 0, p, q) for p, q in zip(a[2:], b[2:])],
+        )
+
+    first = choose(inner, outer)
+    second = choose(outer, inner)
+    eager = jnp.logical_not(first[0])
+    climb0, settle0, drain0 = make_line(first, 1, own, near0, up0, far0, down0)
+    climb1, settle1, drain1 = make_line(second, 4, mid, near1, up1, far1, down1)
 
     def enter(j):
         sibling_copy(j).wait_recv()
@@ -251,14 +250,21 @@
             pl.semaphore_wait(barrier, count)
         loop(lambda j: sibling_copy(j).start(), g * split, (g + 1) * split)
         if g > 0:
-            loop(enter, (g - 1) * split, g * split)
+            @pl.when(eager)
+            def _(g=g):
+                loop(enter, (g - 1) * split, g * split)
+
     loop(lambda i: weight_copy(i).start(), 0, strips)
     hidden_copy.start()
     queries_copy.wait()
     fresh_copy.wait()
     early = problems // 2
     local_part(0)
-    loop(enter, chunks - split, chunks)
+
+    @pl.when(eager)
+    def _():
+        loop(enter, chunks - split, chunks)
+
     for p in range(1, early):
         local_part(p)
 
@@ -418,20 +424,26 @@
         return jnp.logical_and(at >= 0, at < length)
 
     def advance(i):
-        @pl.when(i < chunks)
+        @pl.when(jnp.logical_and(first[0], i < chunks))
         def _():
-            turn(i)
+            enter(i)
+
+        j = i - jnp.where(first[0], LAG_IN, 0)
+
+        @pl.when(within(j, chunks))
+        def _():
+            turn(j)
 
         for p in range(early, problems):
             @pl.when(i == p - early)
             def _(p=p):
                 local_part(p)
 
-        @pl.when(jnp.logical_and(outer[1], within(i - LAG_IN, chunks)))
+        @pl.when(jnp.logical_and(second[0], within(j - LAG_IN, chunks)))
         def _():
-            finish(i - LAG_IN)
-
-        now = i - LAG_OUT
+            finish(j - LAG_IN)
+
+        now = j - jnp.where(core == 0, LAG_OUT, LAG_X if inner_len == 2 else LAG_OUT)
 
         for g in range(groups):
             at = now - g * span
@@ -452,11 +464,11 @@
             def _(g=g):
                 fork_group(g)
 
-        @pl.when(jnp.logical_and(jnp.logical_not(outer[1]), within(now, chunks)))
+        @pl.when(jnp.logical_and(jnp.logical_not(second[0]), within(now, chunks)))
         def _():
             finish(now)
 
-    loop(advance, 0, LAG_OUT + gather_at + (groups - 1) * span + 1)
+    loop(advance, 0, LAG_IN + LAG_OUT + gather_at + (groups - 1) * span + 1)
 
     def rest(j):
         sibling_copy(j).wait_send()
@@ -498,9 +510,6 @@
     smem = pl.BlockSpec(memory_space=pltpu.SMEM)
     hbm = pl.BlockSpec(memory_space=pl.ANY)
     line = pltpu.VMEM((chunks, unit, BLOCK, head_dim), jnp.bfloat16)
-    none = pltpu.VMEM((1, unit, BLOCK, head_dim), jnp.bfloat16)
-    short = cand_n // 2 // 4 == 2
-    spare = none if short else line
     every = pltpu.VMEM((problems * split, unit, BLOCK, head_dim), jnp.bfloat16)
     stat = pltpu.VMEM((problems, steps * heads, head_dim), jnp.float32)
     dma = pltpu.SemaphoreType.DMA
@@ -517,8 +526,7 @@
             pltpu.VMEM(hidden_in.shape, jnp.bfloat16),
             pltpu.VMEM(hidden_in.shape, jnp.bfloat16),
             every, line, line,
-            spare, spare, line, spare,
-            *[line] * 5,
+            *[line] * 9,
             every, stat, stat, stat,
             pltpu.VMEM((GROUP * steps * heads, head_dim), jnp.float32),
             pltpu.VMEM((2, groups, heads // 2, 2 * rows, 2 * head_dim), jnp.bfloat16),

time: 48.4 us -> 46.8 us (0.967)
  Pallas kernels: 46.3 us -> 44.8 us
    pallas_call x1, Pallas kernels: 46.3 us -> 44.8 us  [local(): pl.pallas_call(functools.partial(kernel, cand_n, tp_n, tile, split), out_...]
where the time goes in v4:
time: 46.8 us; the launch traced here: 46.7 us
  Pallas kernels  44.8 us (96%)
  local copies, waits for them, and re-layouts  1.83 us (4%)
    pallas_call x1, Pallas kernels, local(): pl.pallas_call(functools.partial(kernel, cand_n, tp_n, tile, split), out_...  44.8 us
    unnamed x1, local copies, waits for them, and re-layouts  1.83 us

profile of v4, /device:TPU:0, one launch (start us, length us, event | category | flops | bytes accessed | tf_op | source)
XLA Modules:
  0.0 46.7 jit_solution(5365913415458280426)
XLA Ops:
  0.0 44.8 %shard_map.82 = bf16[8,2,8192]{2,1,0:T(2,128)(2,1)} custom-call(s32[8]{0:T(128)} %lengths.1, s32[8]{0:T(128)} %winner.1, f32[16,64]{1,0:T(8,128)} %scales.1, bf16[8,32,128]{2,1,0:T(8,128)(2,1)} %bitcast.2, bf16[8,16,128]{2,1,0:T(8,128)(2,1)} %bitcast.3, bf16[8,2,8192]{2,1,0:T(2,128)(2,1)} %hidden_hbm.1, bf16[8,4,2,512,128]{4,3,2,1,0:T(8,128)(2,1)} %cache_hbm.1, ...), custom_call_target="tpu_custom_call" | custom-call | tf_op jit(solution)/shard_map/pallas_call | solution.py:516
  44.8 1.8 %copy.10 = bf16[8,2,8192]{2,1,0:T(2,128)(2,1)} copy(bf16[8,2,8192]{2,1,0:T(2,128)(2,1)} %shard_map.82) | data formatting | bytes 524288
